TPU v7x, 256 devices: a whole 4x4x8 slice. The times are simulated.
256 devices in a mesh: prow: 32 (over z, y), pcol: 8 (over x, core).
Axes of the slice: x: 4, y: 4, z: 8, core: 2. Of those that a mesh axis runs over, the one named last changes fastest.
Arguments:
- right_side: bfloat16 [3, 32, 256, 128], P(None, 'prow'), may hold values from -6 to 6
- lower_blocks: bfloat16 [3, 32, 256, 8192], P(None, 'prow', None, 'pcol'), may hold values from -0.0625 to 0.0625
- upper_blocks: bfloat16 [3, 32, 256, 8192], P(None, 'prow', None, 'pcol'), may hold values from -0.0625 to 0.0625
- lower_inverse: bfloat16 [3, 32, 256, 256], P(None, 'prow'), as said below
- upper_inverse: bfloat16 [3, 32, 256, 256], P(None, 'prow'), as said below
- pattern: int32 [3, 32, 32], replicated, may hold values 0 or 1
Outputs:
- solution: bfloat16 [3, 32, 256, 128], P(None, 'prow')
Inputs may be any that keep to these rules, and one draw needn't show every extreme that they name: `lower_inverse`: each block is lower triangular with its diagonal between 0.6 and 1.4. `upper_inverse`: each block is upper triangular with its diagonal between 0.6 and 1.4.
All inputs are finite; a program needn't handle non-finite values.
Results may differ from a plain program's by a relative error of at most 0.007.
Values may be sent and summed in bfloat16 or wider, within the bound.
A program may use at most 64 MiB of HBM per device.

v0:
```python
import jax
import jax.numpy as jnp
from jax import lax
from jax.sharding import PartitionSpec as P


def pair_index(later, earlier):
    return later * (later - 1) // 2 + earlier


def settle(partial_value, base_rhs, inverse):
    matrix = inverse.astype(jnp.float32)
    if partial_value is None:
        return jnp.dot(matrix, base_rhs, precision=lax.Precision.HIGHEST).astype(jnp.bfloat16)
    summed = lax.psum(partial_value, "pcol")
    return jnp.dot(matrix, base_rhs - summed, precision=lax.Precision.HIGHEST).astype(jnp.bfloat16)


def collect(values, first_col, group_size):
    gathered = lax.all_gather(values[None], "prow", axis=0, tiled=True)
    return lax.dynamic_slice_in_dim(gathered, first_col, group_size, 0)


def body(right_side, lower_blocks, upper_blocks, lower_inverse, upper_inverse, pattern):
    levels = right_side.shape[0]
    block_size = right_side.shape[2]
    width_cols = right_side.shape[3]
    group_size = lower_blocks.shape[3] // block_size
    row_index = lax.axis_index("prow")
    col_index = lax.axis_index("pcol")
    first_col = col_index * group_size
    solved = [None] * levels
    fetched = [None] * levels
    for level_now in range(levels):
        partial_value = None
        for earlier in range(level_now):
            pair_now = pair_index(level_now, earlier)
            keep_mask = lax.dynamic_slice(
                pattern[pair_now], (row_index, first_col), (1, group_size)
            )[0]
            masked = fetched[earlier] * keep_mask.astype(jnp.bfloat16)[:, None, None]
            product = jnp.dot(
                lower_blocks[pair_now, 0],
                masked.reshape(group_size * block_size, width_cols),
                preferred_element_type=jnp.float32,
            )
            partial_value = product if partial_value is None else partial_value + product
        solved[level_now] = settle(
            partial_value, right_side[level_now, 0].astype(jnp.float32), lower_inverse[level_now, 0]
        )
        if level_now + 1 < levels:
            fetched[level_now] = collect(solved[level_now], first_col, group_size)
    results = [None] * levels
    fetched = [None] * levels
    for level_now in reversed(range(levels)):
        partial_value = None
        for later in range(level_now + 1, levels):
            pair_now = pair_index(later, level_now)
            keep_mask = lax.dynamic_slice(
                pattern[pair_now], (first_col, row_index), (group_size, 1)
            )[:, 0]
            masked = fetched[later] * keep_mask.astype(jnp.bfloat16)[:, None, None]
            product = jnp.dot(
                upper_blocks[pair_now, 0],
                masked.reshape(group_size * block_size, width_cols),
                preferred_element_type=jnp.float32,
            )
            partial_value = product if partial_value is None else partial_value + product
        results[level_now] = settle(
            partial_value, solved[level_now].astype(jnp.float32), upper_inverse[level_now, 0]
        )
        if level_now > 0:
            fetched[level_now] = collect(results[level_now], first_col, group_size)
    return jnp.stack(results)[:, None]


def solution(mesh):
    placed = (
        P(None, "prow", None, None),
        P(None, "prow", None, "pcol"),
        P(None, "prow", None, "pcol"),
        P(None, "prow", None, None),
        P(None, "prow", None, None),
        P(),
    )
    return jax.shard_map(
        body, mesh=mesh, in_specs=placed, out_specs=P(None, "prow", None, None), check_vma=False
    )
```

profile of v0, /device:TPU:1, one launch (start us, length us, event | category | flops | bytes accessed | tf_op | source)
XLA Modules:
  0.0 596.3 jit_solution(6616621899532533295)
XLA Ops:
  6.5 1.8 convolution_convert_fusion.5
  8.3 0.0 all-gather.9.cloned.1.call-update
  8.3 0.0 all-reduce.5.cloned.1.call-start
  8.4 0.8 fusion.52
  9.2 0.1 fusion.47
  9.2 77.9 %all-gather.9.cloned.1.call-done = bf16[8192,128]{1,0:T(8,128)(2,1)} async-done(((bf16[256,128]{1,0:T(8,128)(2,1)}), bf16[8192,128]{1,0:T(8,128)(2,1)}) %all-gather.9.cloned.1.call-update) | async-done | bytes 2097168 | tf_op jit(solution)/shard_map/all_gather | solution.py:20
  87.1 1.1 dynamic-slice_multiply_fusion.2
  88.1 2.0 convolution_bitcast_fusion
  90.1 0.0 all-reduce.5.cloned.1.call-update
  90.2 0.0 all-gather.11.cloned.1.call-start
  90.2 64.8 %all-reduce.5.cloned.1.call-done = f32[256,128]{1,0:T(8,128)} async-done(((f32[256,128]{1,0:T(8,128)}), f32[256,128]{1,0:T(8,128)}) %all-reduce.5.cloned.1.call-update) | async-done | bytes 131088 | tf_op jit(solution)/shard_map/psum | solution.py:15
  155.1 1.8 fusion.2
  156.9 0.0 all-gather.11.cloned.1.call-update
  156.9 0.0 all-reduce.7.cloned.1.call-start
  157.0 0.1 fusion.51
  157.0 72.7 %all-gather.11.cloned.1.call-done = bf16[8192,128]{0,1:T(8,128)(2,1)} async-done(((bf16[256,128]{0,1:T(8,128)(2,1)}), bf16[8192,128]{0,1:T(8,128)(2,1)}) %all-gather.11.cloned.1.call-update) | async-done | bytes 2097168 | tf_op jit(solution)/shard_map/all_gather | solution.py:20
  229.7 2.3 copy.8
  232.0 0.2 dynamic-slice_multiply_fusion.1
  232.3 0.3 fusion.8
  232.6 0.9 fusion
  233.6 0.0 all-reduce.7.cloned.1.call-update
  233.6 0.0 all-gather.13.cloned.1.call-start
  233.6 65.6 %all-reduce.7.cloned.1.call-done = f32[256,128]{1,0:T(8,128)} async-done(((f32[256,128]{1,0:T(8,128)}), f32[256,128]{1,0:T(8,128)}) %all-reduce.7.cloned.1.call-update) | async-done | bytes 131088 | tf_op jit(solution)/shard_map/psum | solution.py:15
  299.3 1.2 convolution_convert_fusion.3
  300.5 0.8 convolution_convert_fusion.2
  301.3 0.0 all-gather.13.cloned.1.call-update
  301.3 0.0 all-reduce.9.cloned.1.call-start
  301.4 0.2 fusion.45
  301.6 0.2 fusion.43
  301.8 72.0 %all-gather.13.cloned.1.call-done = bf16[8192,128]{0,1:T(8,128)(2,1)} async-done(((bf16[256,128]{0,1:T(8,128)(2,1)}), bf16[8192,128]{0,1:T(8,128)(2,1)}) %all-gather.13.cloned.1.call-update) | async-done | bytes 2097168 | tf_op jit(solution)/shard_map/all_gather | solution.py:20
  373.8 2.3 copy.10
  376.1 0.3 dynamic-slice_multiply_fusion.4
  376.5 1.0 convolution_bitcast_fusion.1
  377.4 0.0 all-reduce.9.cloned.1.call-update
  377.5 0.0 all-gather.15.cloned.1.call-start
  377.5 65.6 %all-reduce.9.cloned.1.call-done = f32[256,128]{0,1:T(8,128)} async-done(((f32[256,128]{0,1:T(8,128)}), f32[256,128]{0,1:T(8,128)}) %all-reduce.9.cloned.1.call-update) | async-done | bytes 131088 | tf_op jit(solution)/shard_map/psum | solution.py:15
  443.1 1.8 convolution_convert_fusion.1
  445.0 0.0 all-gather.15.cloned.1.call-update
  445.0 0.0 all-reduce.11.cloned.1.call-start
  445.1 72.7 %all-gather.15.cloned.1.call-done = bf16[8192,128]{0,1:T(8,128)(2,1)} async-done(((bf16[256,128]{0,1:T(8,128)(2,1)}), bf16[8192,128]{0,1:T(8,128)(2,1)}) %all-gather.15.cloned.1.call-update) | async-done | bytes 2097168 | tf_op jit(solution)/shard_map/all_gather | solution.py:20
  517.8 2.2 copy.12
  520.0 0.2 dynamic-slice_multiply_fusion
  520.3 0.3 fusion.5
  520.6 1.0 fusion.1
  521.6 0.0 all-reduce.11.cloned.1.call-update
  521.6 65.8 %all-reduce.11.cloned.1.call-done = f32[256,128]{1,0:T(8,128)} async-done(((f32[256,128]{1,0:T(8,128)}), f32[256,128]{1,0:T(8,128)}) %all-reduce.11.cloned.1.call-update) | async-done | bytes 131088 | tf_op jit(solution)/shard_map/psum | solution.py:15
  587.4 1.2 fusion.3
  588.6 0.8 copy.7
  (24 shorter events, 0.2 us)
Async XLA Ops:
  6.5 148.5 %copy-start.7 = (bf16[3,1,256,256]{3,2,1,0:T(8,128)(2,1)S(1)}, bf16[3,1,256,256]{3,2,1,0:T(8,128)(2,1)}, u32[]{:S(2)}) copy-start(bf16[3,1,256,256]{3,2,1,0:T(8,128)(2,1)} %param.9) | copy-start | bytes 1179652
  6.5 148.5 %copy-start.8 = (bf16[3,1,256,128]{3,2,1,0:T(8,128)(2,1)S(1)}, bf16[3,1,256,128]{3,2,1,0:T(8,128)(2,1)}, u32[]{:S(2)}) copy-start(bf16[3,1,256,128]{3,2,1,0:T(8,128)(2,1)} %param.6) | copy-start | bytes 589828
  6.5 80.5 %all-gather.9.cloned.1.call-start = ((), (), s32[]{:S(2)}) async-start(), calls=%async_computation.4 | async-start | bytes 2162688 | tf_op jit(solution)/shard_map/all_gather | solution.py:20
  8.3 146.7 %all-reduce.5.cloned.1.call-start = ((), (), s32[]{:S(2)}) async-start(), calls=%async_computation | async-start | bytes 262144 | tf_op jit(solution)/shard_map/psum | solution.py:15
  90.2 139.6 %all-gather.11.cloned.1.call-start = ((), (), s32[]{:S(2)}) async-start(), calls=%async_computation.5 | async-start | bytes 2162688 | tf_op jit(solution)/shard_map/all_gather | solution.py:20
  156.9 142.4 %all-reduce.7.cloned.1.call-start = ((), (), s32[]{:S(2)}) async-start(), calls=%async_computation.1 | async-start | bytes 262144 | tf_op jit(solution)/shard_map/psum | solution.py:15
  229.7 2.6 copy-start.1
  232.3 68.2 %copy-start.5 = (bf16[3,1,256,256]{3,2,1,0:T(8,128)(2,1)S(1)}, bf16[3,1,256,256]{3,2,1,0:T(8,128)(2,1)}, u32[]{:S(2)}) copy-start(bf16[3,1,256,256]{3,2,1,0:T(8,128)(2,1)} %param.10) | copy-start | bytes 1179652
  233.6 140.2 %all-gather.13.cloned.1.call-start = ((), (), s32[]{:S(2)}) async-start(), calls=%async_computation.6 | async-start | bytes 2162688 | tf_op jit(solution)/shard_map/all_gather | solution.py:20
  301.3 141.8 %all-reduce.9.cloned.1.call-start = ((), (), s32[]{:S(2)}) async-start(), calls=%async_computation.2 | async-start | bytes 262144 | tf_op jit(solution)/shard_map/psum | solution.py:15
  373.8 2.6 copy-start
  376.1 67.0 %copy-start.3 = (bf16[256,128]{0,1:T(8,128)(2,1)S(1)}, bf16[256,128]{0,1:T(8,128)(2,1)}, u32[]{:S(2)}) copy-start(bf16[256,128]{0,1:T(8,128)(2,1)} %fusion.2) | copy-start | bytes 196612
  377.5 140.4 %all-gather.15.cloned.1.call-start = ((), (), s32[]{:S(2)}) async-start(), calls=%async_computation.7 | async-start | bytes 2162688 | tf_op jit(solution)/shard_map/all_gather | solution.py:20
  445.0 142.4 %all-reduce.11.cloned.1.call-start = ((), (), s32[]{:S(2)}) async-start(), calls=%async_computation.3 | async-start | bytes 262144 | tf_op jit(solution)/shard_map/psum | solution.py:15
  520.0 67.4 %copy-start.6 = (bf16[256,128]{1,0:T(8,128)(2,1)S(1)}, bf16[256,128]{1,0:T(8,128)(2,1)}, u32[]{:S(2)}) copy-start(bf16[256,128]{1,0:T(8,128)(2,1)} %convolution_convert_fusion.5) | copy-start | bytes 196612
  520.2 68.3 %copy-start.2 = (bf16[128,256]{1,0:T(8,128)(2,1)S(1)}, bf16[128,256]{1,0:T(8,128)(2,1)}, u32[]{:S(2)}) copy-start(bf16[128,256]{1,0:T(8,128)(2,1)} %convolution_convert_fusion.2) | copy-start | bytes 196612
  520.2 68.3 %copy-start.4 = (bf16[128,256]{1,0:T(8,128)(2,1)S(1)}, bf16[128,256]{1,0:T(8,128)(2,1)}, u32[]{:S(2)}) copy-start(bf16[128,256]{1,0:T(8,128)(2,1)} %convolution_convert_fusion.1) | copy-start | bytes 196612
Sparse Core Ops, SparseCore 0:
  9.9 77.1 all-gather.8
  90.3 64.7 all-reduce.4
  157.5 72.1 all-gather.10
  233.7 65.5 all-reduce.6
  301.6 72.1 all-gather.12
  377.6 65.5 all-reduce.8
  445.6 72.1 all-gather.14
  521.7 65.5 all-reduce.10
where the time goes:
time: 598 us; the launch traced here: 596 us
  waiting for transfers between devices  557 us (93%)
  matrix products  14.2 us (2%)
  between operations  13.7 us (2%)
  local copies, waits for them, and re-layouts  8.51 us (1%)
    all_gather x4, waiting for transfers between devices, collect(): gathered = lax.all_gather(values[None], 'prow', axis=0, tiled=True)  295 us
    psum x4, waiting for transfers between devices, settle(): summed = lax.psum(partial_value, 'pcol')  262 us
  transfers between devices with their start and end apart: 8, of which 8 were waited for; matrix products, arithmetic and copies ran while one was open for 0% of the time, Pallas kernels for 0%

commit v1 on v0

v1 whole, which is shorter than its diff:
```python
import functools

import jax
import jax.numpy as jnp
from jax import lax
from jax.experimental import pallas as pl
from jax.experimental.pallas import tpu as pltpu
from jax.sharding import PartitionSpec as P

MESH = pl.DeviceIdType.MESH
F32 = jnp.float32
BF16 = jnp.bfloat16


def mm(a, b):
    return jnp.dot(a, b, preferred_element_type=F32)


def kernel(
    n_rows, n_cols, n_group,
    rhs_hbm, low_hbm, upp_hbm, linv_hbm, uinv_hbm, pat_hbm,
    out_hbm,
    rhs, low, upp, linv, uinv, pat,
    first, base1, base2, base0, carry, prod, land, slices, fetched, padded, n_hi, n_lo,
    load_sem, pat_sem, cast_send, cast_recv, sum_send, sum_recv, out_send, out_recv,
):
    size = rhs.shape[1]
    part = size // n_cols
    row = lax.axis_index("prow")
    col = lax.axis_index("pcol")
    owner_col = row // n_group
    place = row % n_group
    n_outer = n_rows // n_group

    barrier = pltpu.get_barrier_semaphore()

    def target_row(step):
        i, j = step // n_group, step % n_group
        d_outer = n_outer // 2 + ((i + 1) // 2) * (1 - 2 * (i % 2))
        d_inner = n_group // 2 + ((j + 1) // 2) * (1 - 2 * (j % 2))
        outer = (row // n_group + d_outer) % n_outer
        inner = (row % n_group + d_inner) % n_group
        return outer * n_group + inner

    is_own = owner_col == col

    for q in range(n_cols):
        for b in range(n_group):
            src_row = col * n_group + b
            if True:
                other = jnp.logical_or(src_row != row, q != col)

                @pl.when(other)
                def _():
                    pl.semaphore_signal(barrier, inc=1, device_id=(src_row, q), device_id_type=MESH)

        @pl.when(q != col)
        def _():
            pl.semaphore_signal(barrier, inc=1, device_id=(row, q), device_id_type=MESH)

    loads = [
        pltpu.make_async_copy(linv_hbm.at[:, 0], linv, load_sem.at[0]),
        pltpu.make_async_copy(rhs_hbm.at[:, 0], rhs, load_sem.at[1]),
        pltpu.make_async_copy(pat_hbm, pat, pat_sem),
        pltpu.make_async_copy(low_hbm.at[0, 0], low.at[0], load_sem.at[2]),
        pltpu.make_async_copy(uinv_hbm.at[:, 0], uinv, load_sem.at[3]),
        pltpu.make_async_copy(low_hbm.at[1, 0], low.at[1], load_sem.at[4]),
        pltpu.make_async_copy(low_hbm.at[2, 0], low.at[2], load_sem.at[5]),
        pltpu.make_async_copy(upp_hbm.at[:, 0], upp, load_sem.at[6]),
    ]
    for copy in loads:
        copy.start()

    own_rows = pl.ds(pl.multiple_of(col * part, part), part)

    def cast_copy(rnd, step):
        source = first.at[own_rows] if rnd == 0 else slices.at[rnd]
        where = pl.ds(pl.multiple_of(place * size + col * part, part), part)
        return pltpu.make_async_remote_copy(
            src_ref=source,
            dst_ref=fetched.at[rnd, where],
            send_sem=cast_send.at[rnd],
            recv_sem=cast_recv.at[rnd],
            device_id=(target_row(step), owner_col),
            device_id_type=MESH,
        )

    def cast_local(rnd):
        source = first.at[own_rows] if rnd == 0 else slices.at[rnd]
        where = pl.ds(pl.multiple_of(place * size + col * part, part), part)
        return pltpu.make_async_copy(source, fetched.at[rnd, where], cast_recv.at[rnd])

    def cast_start(rnd):
        def one(step, unused):
            cast_copy(rnd, step).start()
            return unused

        lax.fori_loop(0, n_rows - 1, one, 0)

        @pl.when(jnp.logical_not(is_own))
        def _():
            cast_copy(rnd, n_rows - 1).start()

        @pl.when(is_own)
        def _():
            cast_local(rnd).start()

    def cast_wait(rnd):
        pltpu.make_async_copy(fetched.at[rnd], fetched.at[rnd], cast_recv.at[rnd]).wait()

    def cast_drain(rnd):
        def one(step, unused):
            cast_copy(rnd, step).wait_send()
            return unused

        lax.fori_loop(0, n_rows - 1, one, 0)

        @pl.when(jnp.logical_not(is_own))
        def _():
            cast_copy(rnd, n_rows - 1).wait_send()

    def peer(step):
        return lax.rem(col + step, n_cols)

    def sum_copy(rnd, step):
        q = peer(step)
        return pltpu.make_async_remote_copy(
            src_ref=prod.at[rnd, pl.ds(pl.multiple_of(q * part, part), part)],
            dst_ref=land.at[rnd, col],
            send_sem=sum_send.at[rnd],
            recv_sem=sum_recv.at[rnd],
            device_id=(row, q),
            device_id_type=MESH,
        )

    order = [4, 3, 5, 2, 6, 1, 7]

    def scatter(rnd, value):
        prod[rnd] = value
        for step in order:
            sum_copy(rnd, step).start()
        land[rnd, col] = prod[rnd, own_rows]

    def summed(rnd):
        pltpu.make_async_copy(
            land.at[rnd, pl.ds(0, n_cols - 1)], land.at[rnd, pl.ds(0, n_cols - 1)], sum_recv.at[rnd]
        ).wait()
        total = land[rnd, 0]
        for q in range(1, n_cols):
            total = total + land[rnd, q]
        return total

    def out_copy(rnd, level, step):
        return pltpu.make_async_remote_copy(
            src_ref=slices.at[rnd],
            dst_ref=out_hbm.at[level, 0, own_rows],
            send_sem=out_send.at[level],
            recv_sem=out_recv.at[level],
            device_id=(row, peer(step)),
            device_id_type=MESH,
        )

    def share(rnd, level):
        for step in order:
            out_copy(rnd, level, step).start()
        pltpu.make_async_copy(slices.at[rnd], out_hbm.at[level, 0, own_rows], out_recv.at[level]).start()

    def share_wait(rnd, level):
        pltpu.make_async_copy(out_hbm.at[level, 0], out_hbm.at[level, 0], out_recv.at[level]).wait()
        for step in order:
            out_copy(rnd, level, step).wait_send()

    def fold_lower(pair, products):
        for b in range(n_group):
            cols = slice(b * size, (b + 1) * size)
            keep = pat[pair, row, col * n_group + b].astype(F32)
            low[pair, :, cols] = (products(low[pair, :, cols]) * keep).astype(BF16)

    def fold_upper(pair, level):
        for b in range(n_group):
            cols = slice(b * size, (b + 1) * size)
            keep = pat[pair, col * n_group + b, row].astype(F32)
            upp[pair, :, cols] = (mm(uinv[level], upp[pair, :, cols]) * keep).astype(BF16)

    loads[0].wait()
    loads[1].wait()
    first[...] = mm(linv[0], rhs[0]).astype(BF16)

    pl.semaphore_wait(barrier, n_rows + n_cols - 1 - is_own.astype(jnp.int32))
    cast_start(0)

    loads[2].wait()
    loads[3].wait()
    fold_lower(0, lambda block: mm(linv[1], block))
    base1[...] = mm(linv[1], rhs[1])
    loads[4].wait()
    both = mm(uinv[2], linv[2])
    n_hi[...] = both.astype(BF16)
    n_lo[...] = (both - n_hi[...].astype(F32)).astype(BF16)

    def through(block):
        return mm(n_hi[...], block) + mm(n_lo[...], block)

    base2[...] = through(rhs[2])
    base0[...] = mm(uinv[0], first[...])
    loads[5].wait()
    fold_lower(1, through)
    loads[6].wait()
    fold_lower(2, through)

    cast_wait(0)
    scatter(0, mm(low[0], fetched[0]))
    carry[...] = mm(low[1], fetched[0])
    slices[1] = (base1[own_rows] - summed(0)).astype(BF16)
    cast_start(1)

    loads[7].wait()
    fold_upper(2, 1)
    fold_upper(1, 0)
    fold_upper(0, 0)
    padded[...] = jnp.zeros_like(padded)
    padded[own_rows] = slices[1]

    cast_wait(1)
    scatter(1, carry[...] + mm(low[2], fetched[1]))
    carry[...] = mm(uinv[1], padded[...])
    slices[2] = (base2[own_rows] - summed(1)).astype(BF16)
    cast_start(2)
    share(2, 2)

    cast_wait(2)
    scatter(2, mm(upp[2], fetched[2]) - carry[...])
    carry[...] = mm(upp[1], fetched[2])
    slices[3] = (-summed(2)).astype(BF16)
    cast_start(3)
    share(3, 1)

    cast_wait(3)
    scatter(3, carry[...] + mm(upp[0], fetched[3]))
    slices[4] = (base0[own_rows] - summed(3)).astype(BF16)
    share(4, 0)

    for rnd in range(4):
        cast_drain(rnd)
        for step in order:
            sum_copy(rnd, step).wait_send()
    share_wait(2, 2)
    share_wait(3, 1)
    share_wait(4, 0)


def solution(mesh):
    n_rows, n_cols = mesh.shape["prow"], mesh.shape["pcol"]

    def body(right_side, lower_blocks, upper_blocks, lower_inverse, upper_inverse, pattern):
        levels, _, size, width = right_side.shape
        pairs, _, _, span = lower_blocks.shape
        n_group = span // size
        part = size // n_cols
        any_spec = pl.BlockSpec(memory_space=pl.ANY)
        return pl.pallas_call(
            functools.partial(kernel, n_rows, n_cols, n_group),
            out_shape=jax.ShapeDtypeStruct((levels, 1, size, width), BF16),
            in_specs=[any_spec] * 6,
            out_specs=any_spec,
            scratch_shapes=[
                pltpu.VMEM((levels, size, width), BF16),
                pltpu.VMEM((pairs, size, span), BF16),
                pltpu.VMEM((pairs, size, span), BF16),
                pltpu.VMEM((levels, size, size), BF16),
                pltpu.VMEM((levels, size, size), BF16),
                pltpu.SMEM(pattern.shape, jnp.int32),
                pltpu.VMEM((size, width), BF16),
                pltpu.VMEM((size, width), F32),
                pltpu.VMEM((size, width), F32),
                pltpu.VMEM((size, width), F32),
                pltpu.VMEM((size, width), F32),
                pltpu.VMEM((4, size, width), F32),
                pltpu.VMEM((4, n_cols, part, width), F32),
                pltpu.VMEM((5, part, width), BF16),
                pltpu.VMEM((4, span, width), BF16),
                pltpu.VMEM((size, width), BF16),
                pltpu.VMEM((size, size), BF16),
                pltpu.VMEM((size, size), BF16),
                pltpu.SemaphoreType.DMA((7,)),
                pltpu.SemaphoreType.DMA(()),
                pltpu.SemaphoreType.DMA((4,)),
                pltpu.SemaphoreType.DMA((4,)),
                pltpu.SemaphoreType.DMA((4,)),
                pltpu.SemaphoreType.DMA((4,)),
                pltpu.SemaphoreType.DMA((3,)),
                pltpu.SemaphoreType.DMA((3,)),
            ],
            compiler_params=pltpu.CompilerParams(collective_id=0, has_side_effects=True),
        )(right_side, lower_blocks, upper_blocks, lower_inverse, upper_inverse, pattern)

    placed = (
        P(None, "prow", None, None),
        P(None, "prow", None, "pcol"),
        P(None, "prow", None, "pcol"),
        P(None, "prow", None, None),
        P(None, "prow", None, None),
        P(),
    )
    return jax.shard_map(
        body, mesh=mesh, in_specs=placed, out_specs=P(None, "prow", None, None), check_vma=False
    )
```

time: 598 us -> 73.2 us (0.12)
  waiting for transfers between devices: 557 us -> 0 us
  Pallas kernels: 0 us -> 71.5 us
  matrix products: 14.2 us -> 0 us
  between operations: 13.7 us -> 0.01 us
  local copies, waits for them, and re-layouts: 8.51 us -> 1.62 us
    all_gather x4 -> x0, waiting for transfers between devices: 295 us -> none  [collect(): gathered = lax.all_gather(values[None], 'prow', axis=0, tiled=True)]
    psum x4 -> x0, waiting for transfers between devices: 262 us -> none  [settle(): summed = lax.psum(partial_value, 'pcol')]
    pallas_call x0 -> x1, Pallas kernels: none -> 71.5 us  [body(): pl.pallas_call(functools.partial(kernel, n_rows, n_cols, n_group), out_sh...]
    dot_general x12 -> x0, matrix products: 14.2 us -> none  [the longest x4 6.07 us: settle(): jnp.dot(matrix, base_rhs - summed, precision=lax.Precision.HIGHEST)]
  transfers between devices with their start and end apart: 8 -> 0, of which waited for: 8 -> 0; matrix products, arithmetic and copies ran while one was open for 0% -> 0% of each run, Pallas kernels for 0% -> 0%
where the time goes in v1:
time: 73.2 us; the launch traced here: 73.1 us
  Pallas kernels  71.5 us (98%)
  local copies, waits for them, and re-layouts  1.62 us (2%)
    pallas_call x1, Pallas kernels, body(): pl.pallas_call(functools.partial(kernel, n_rows, n_cols, n_group), out_sh...  71.5 us
    unnamed x1, local copies, waits for them, and re-layouts  1.62 us

profile of v1, /device:TPU:1, one launch (start us, length us, event | category | flops | bytes accessed | tf_op | source)
XLA Modules:
  0.0 73.1 jit_solution(18232985031096436139)
XLA Ops:
  0.0 71.5 %shard_map.64 = bf16[3,1,256,128]{3,2,1,0:T(8,128)(2,1)} custom-call(bf16[3,1,256,128]{3,2,1,0:T(8,128)(2,1)} %rhs_hbm.1, bf16[3,1,256,1024]{3,2,1,0:T(8,128)(2,1)} %low_hbm.1, bf16[3,1,256,1024]{3,2,1,0:T(8,128)(2,1)} %upp_hbm.1, bf16[3,1,256,256]{3,2,1,0:T(8,128)(2,1)} %linv_hbm.1, bf16[3,1,256,256]{3,2,1,0:T(8,128)(2,1)} %uinv_hbm.1, s32[3,32,32]{2,1,0:T(8,128)} %pat_hbm.1), custom_call_target="tpu_custom_call" | custom-call | tf_op jit(solution)/shard_map/pallas_call | solution.py:261
  71.5 1.6 %copy.8 = bf16[3,1,256,128]{3,2,1,0:T(8,128)(2,1)} copy(bf16[3,1,256,128]{3,2,1,0:T(8,128)(2,1)} %shard_map.64) | data formatting | bytes 393216

commit v2 on v1

--- a/solution.py
+++ b/solution.py
@@ -136,7 +136,7 @@
     order = [4, 3, 5, 2, 6, 1, 7]
 
     def scatter(rnd, value):
-        prod[rnd] = value
+        prod[rnd] = value.astype(BF16)
         for step in order:
             sum_copy(rnd, step).start()
         land[rnd, col] = prod[rnd, own_rows]
@@ -145,9 +145,9 @@
         pltpu.make_async_copy(
             land.at[rnd, pl.ds(0, n_cols - 1)], land.at[rnd, pl.ds(0, n_cols - 1)], sum_recv.at[rnd]
         ).wait()
-        total = land[rnd, 0]
+        total = land[rnd, 0].astype(F32)
         for q in range(1, n_cols):
-            total = total + land[rnd, q]
+            total = total + land[rnd, q].astype(F32)
         return total
 
     def out_copy(rnd, level, step):
@@ -261,7 +261,7 @@
         return pl.pallas_call(
             functools.partial(kernel, n_rows, n_cols, n_group),
             out_shape=jax.ShapeDtypeStruct((levels, 1, size, width), BF16),
-            in_specs=[any_spec] * 6,
+            in_specs=[pl.BlockSpec(memory_space=pltpu.HBM)] * 6,
             out_specs=any_spec,
             scratch_shapes=[
                 pltpu.VMEM((levels, size, width), BF16),
@@ -275,8 +275,8 @@
                 pltpu.VMEM((size, width), F32),
                 pltpu.VMEM((size, width), F32),
                 pltpu.VMEM((size, width), F32),
-                pltpu.VMEM((4, size, width), F32),
-                pltpu.VMEM((4, n_cols, part, width), F32),
+                pltpu.VMEM((4, size, width), BF16),
+                pltpu.VMEM((4, n_cols, part, width), BF16),
                 pltpu.VMEM((5, part, width), BF16),
                 pltpu.VMEM((4, span, width), BF16),
                 pltpu.VMEM((size, width), BF16),
@@ -291,8 +291,8 @@
                 pltpu.SemaphoreType.DMA((3,)),
                 pltpu.SemaphoreType.DMA((3,)),
             ],
-            compiler_params=pltpu.CompilerParams(collective_id=0, has_side_effects=True),
-        )(right_side, lower_blocks, upper_blocks, lower_inverse, upper_inverse, pattern)
+            compiler_params=pltpu.CompilerParams(collective_id=0, has_side_effects=True, vmem_limit_bytes=24 * 1024 * 1024),
+        )(*[pltpu.with_memory_space_constraint(x, pltpu.HBM) for x in (right_side, lower_blocks, upper_blocks, lower_inverse, upper_inverse, pattern)])
 
     placed = (
         P(None, "prow", None, None),

time: 73.2 us -> 70.9 us (0.969)
  Pallas kernels: 71.5 us -> 70.1 us
  local copies, waits for them, and re-layouts: 1.62 us -> 0.68 us
    pallas_call x1, Pallas kernels: 71.5 us -> 70.1 us  [body(): pl.pallas_call(functools.partial(kernel, n_rows, n_cols, n_group), out_sh...]
    unnamed x1, local copies, waits for them, and re-layouts: 1.62 us -> 0.68 us
where the time goes in v2:
time: 70.9 us; the launch traced here: 70.8 us
  Pallas kernels  70.1 us (99%)
    pallas_call x1, Pallas kernels, body(): pl.pallas_call(functools.partial(kernel, n_rows, n_cols, n_group), out_sh...  70.1 us

profile of v2, /device:TPU:1, one launch (start us, length us, event | category | flops | bytes accessed | tf_op | source)
XLA Modules:
  0.0 70.8 jit_solution(14153436647991937844)
XLA Ops:
  0.0 70.1 %shard_map.64 = bf16[3,1,256,128]{3,2,1,0:T(8,128)(2,1)S(1)} custom-call(bf16[3,1,256,128]{3,2,1,0:T(8,128)(2,1)} %rhs_hbm.1, bf16[3,1,256,1024]{3,2,1,0:T(8,128)(2,1)} %low_hbm.1, bf16[3,1,256,1024]{3,2,1,0:T(8,128)(2,1)} %upp_hbm.1, bf16[3,1,256,256]{3,2,1,0:T(8,128)(2,1)} %linv_hbm.1, bf16[3,1,256,256]{3,2,1,0:T(8,128)(2,1)} %uinv_hbm.1, s32[3,32,32]{2,1,0:T(8,128)} %pat_hbm.1), custom_call_target="tpu_custom_call" | custom-call | tf_op jit(solution)/shard_map/pallas_call | solution.py:261
  70.1 0.7 copy.8

commit v3 on v2

--- a/solution.py
+++ b/solution.py
@@ -95,7 +95,8 @@
             cast_copy(rnd, step).start()
             return unused
 
-        lax.fori_loop(0, n_rows - 1, one, 0)
+        for step in range(n_rows - 1):
+            one(step, 0)
 
         @pl.when(jnp.logical_not(is_own))
         def _():
@@ -210,9 +211,9 @@
 
     cast_wait(0)
     scatter(0, mm(low[0], fetched[0]))
-    carry[...] = mm(low[1], fetched[0])
     slices[1] = (base1[own_rows] - summed(0)).astype(BF16)
     cast_start(1)
+    carry[...] = mm(low[1], fetched[0])
 
     loads[7].wait()
     fold_upper(2, 1)
@@ -223,17 +224,17 @@
 
     cast_wait(1)
     scatter(1, carry[...] + mm(low[2], fetched[1]))
-    carry[...] = mm(uinv[1], padded[...])
     slices[2] = (base2[own_rows] - summed(1)).astype(BF16)
     cast_start(2)
     share(2, 2)
+    carry[...] = mm(uinv[1], padded[...])
 
     cast_wait(2)
     scatter(2, mm(upp[2], fetched[2]) - carry[...])
-    carry[...] = mm(upp[1], fetched[2])
     slices[3] = (-summed(2)).astype(BF16)
     cast_start(3)
     share(3, 1)
+    carry[...] = mm(upp[1], fetched[2])
 
     cast_wait(3)
     scatter(3, carry[...] + mm(upp[0], fetched[3]))

time: 70.9 us -> 70.6 us (level)
  no operation moved by 1% of the time
where the time goes in v3:
time: 70.6 us; the launch traced here: 70.5 us
  Pallas kernels  69.8 us (99%)
    pallas_call x1, Pallas kernels, body(): pl.pallas_call(functools.partial(kernel, n_rows, n_cols, n_group), out_sh...  69.8 us

profile of v3, /device:TPU:1, one launch (start us, length us, event | category | flops | bytes accessed | tf_op | source)
XLA Modules:
  0.0 70.5 jit_solution(13733610723027575942)
XLA Ops:
  0.0 69.8 %shard_map.64 = bf16[3,1,256,128]{3,2,1,0:T(8,128)(2,1)S(1)} custom-call(bf16[3,1,256,128]{3,2,1,0:T(8,128)(2,1)} %rhs_hbm.1, bf16[3,1,256,1024]{3,2,1,0:T(8,128)(2,1)} %low_hbm.1, bf16[3,1,256,1024]{3,2,1,0:T(8,128)(2,1)} %upp_hbm.1, bf16[3,1,256,256]{3,2,1,0:T(8,128)(2,1)} %linv_hbm.1, bf16[3,1,256,256]{3,2,1,0:T(8,128)(2,1)} %uinv_hbm.1, s32[3,32,32]{2,1,0:T(8,128)} %pat_hbm.1), custom_call_target="tpu_custom_call" | custom-call | tf_op jit(solution)/shard_map/pallas_call | solution.py:262
  69.8 0.7 copy.8

commit v4 on v3

--- a/solution.py
+++ b/solution.py
@@ -22,7 +22,7 @@
     out_hbm,
     rhs, low, upp, linv, uinv, pat,
     first, base1, base2, base0, carry, prod, land, slices, fetched, padded, n_hi, n_lo,
-    load_sem, pat_sem, cast_send, cast_recv, sum_send, sum_recv, out_send, out_recv,
+    prod_f32, load_sem, pat_sem, cast_send, cast_recv, pass_send, pass_recv, sum_send, sum_recv, out_send, out_recv,
 ):
     size = rhs.shape[1]
     part = size // n_cols
@@ -34,29 +34,30 @@
 
     barrier = pltpu.get_barrier_semaphore()
 
-    def target_row(step):
-        i, j = step // n_group, step % n_group
-        d_outer = n_outer // 2 + ((i + 1) // 2) * (1 - 2 * (i % 2))
-        d_inner = n_group // 2 + ((j + 1) // 2) * (1 - 2 * (j % 2))
-        outer = (row // n_group + d_outer) % n_outer
-        inner = (row % n_group + d_inner) % n_group
-        return outer * n_group + inner
+    near_order = [n_group // 2] + [d for d in range(1, n_group) if d != n_group // 2]
+    outer_order = [4, 3, 5, 2, 6, 1, 7]
+
+    def beside(step):
+        return owner_col * n_group + (place + step) % n_group
+
+    def across(step):
+        return (owner_col + step) % n_outer * n_group + place
 
     is_own = owner_col == col
 
     for q in range(n_cols):
-        for b in range(n_group):
-            src_row = col * n_group + b
-            if True:
-                other = jnp.logical_or(src_row != row, q != col)
-
-                @pl.when(other)
-                def _():
-                    pl.semaphore_signal(barrier, inc=1, device_id=(src_row, q), device_id_type=MESH)
+        src_row = col * n_group + place
+
+        @pl.when(jnp.logical_or(src_row != row, q != col))
+        def _():
+            pl.semaphore_signal(barrier, inc=1, device_id=(src_row, q), device_id_type=MESH)
 
         @pl.when(q != col)
         def _():
             pl.semaphore_signal(barrier, inc=1, device_id=(row, q), device_id_type=MESH)
+
+    for step in near_order:
+        pl.semaphore_signal(barrier, inc=1, device_id=(beside(step), col), device_id_type=MESH)
 
     loads = [
         pltpu.make_async_copy(linv_hbm.at[:, 0], linv, load_sem.at[0]),
@@ -73,52 +74,83 @@
 
     own_rows = pl.ds(pl.multiple_of(col * part, part), part)
 
+    block_rows = pl.ds(pl.multiple_of(place * size, size), size)
+
+    def cast_ends(rnd):
+        source = first.at[own_rows] if rnd == 0 else slices.at[rnd]
+        return source, fetched.at[rnd, pl.ds(pl.multiple_of(place * size + col * part, part), part)]
+
     def cast_copy(rnd, step):
-        source = first.at[own_rows] if rnd == 0 else slices.at[rnd]
-        where = pl.ds(pl.multiple_of(place * size + col * part, part), part)
+        source, target = cast_ends(rnd)
         return pltpu.make_async_remote_copy(
             src_ref=source,
-            dst_ref=fetched.at[rnd, where],
+            dst_ref=target,
             send_sem=cast_send.at[rnd],
-            recv_sem=cast_recv.at[rnd],
-            device_id=(target_row(step), owner_col),
+            recv_sem=cast_recv.at[rnd, col],
+            device_id=(across(step), owner_col),
             device_id_type=MESH,
         )
 
-    def cast_local(rnd):
-        source = first.at[own_rows] if rnd == 0 else slices.at[rnd]
-        where = pl.ds(pl.multiple_of(place * size + col * part, part), part)
-        return pltpu.make_async_copy(source, fetched.at[rnd, where], cast_recv.at[rnd])
-
     def cast_start(rnd):
-        def one(step, unused):
+        for step in outer_order:
             cast_copy(rnd, step).start()
-            return unused
-
-        for step in range(n_rows - 1):
-            one(step, 0)
 
         @pl.when(jnp.logical_not(is_own))
         def _():
-            cast_copy(rnd, n_rows - 1).start()
+            cast_copy(rnd, 0).start()
 
         @pl.when(is_own)
         def _():
-            cast_local(rnd).start()
-
-    def cast_wait(rnd):
-        pltpu.make_async_copy(fetched.at[rnd], fetched.at[rnd], cast_recv.at[rnd]).wait()
+            source, target = cast_ends(rnd)
+            pltpu.make_async_copy(source, target, cast_recv.at[rnd, col]).start()
+
+    def pass_copy(rnd, chip, step):
+        rows = fetched.at[rnd, pl.ds(pl.multiple_of(place * size + chip * 2 * part, part), 2 * part)]
+        return pltpu.make_async_remote_copy(
+            src_ref=rows,
+            dst_ref=rows,
+            send_sem=pass_send.at[rnd],
+            recv_sem=pass_recv.at[rnd, step],
+            device_id=(beside(step), col),
+            device_id_type=MESH,
+        )
+
+    def chip_at(d):
+        return (col // 2 + d) % (n_cols // 2)
+
+    def relay(rnd):
+        for d in (0, 1, 3, 2):
+            chip = chip_at(d)
+            for k in range(2):
+                q = chip * 2 + k
+                rows = fetched.at[rnd, pl.ds(pl.multiple_of(place * size + q * part, part), part)]
+                pltpu.make_async_copy(rows, rows, cast_recv.at[rnd, q]).wait()
+            for step in near_order:
+                pass_copy(rnd, chip, step).start()
+
+    def product(rnd, matrix):
+        def piece(offset):
+            where = pl.ds(pl.multiple_of((place + offset) % n_group * size, size), size)
+            return mm(matrix[:, where], fetched[rnd, where])
+
+        prod_f32[...] = piece(0)
+        for step in (1, 3, 2):
+            where = pl.ds(pl.multiple_of((place + n_group - step) % n_group * size, size), size)
+            pltpu.make_async_copy(fetched.at[rnd, where], fetched.at[rnd, where], pass_recv.at[rnd, step]).wait()
+            prod_f32[...] += piece(n_group - step)
+        return prod_f32[...]
 
     def cast_drain(rnd):
-        def one(step, unused):
+        for step in outer_order:
             cast_copy(rnd, step).wait_send()
-            return unused
-
-        lax.fori_loop(0, n_rows - 1, one, 0)
 
         @pl.when(jnp.logical_not(is_own))
         def _():
-            cast_copy(rnd, n_rows - 1).wait_send()
+            cast_copy(rnd, 0).wait_send()
+
+        for d in range(n_cols // 2):
+            for step in near_order:
+                pass_copy(rnd, d, step).wait_send()
 
     def peer(step):
         return lax.rem(col + step, n_cols)
@@ -187,7 +219,7 @@
     loads[1].wait()
     first[...] = mm(linv[0], rhs[0]).astype(BF16)
 
-    pl.semaphore_wait(barrier, n_rows + n_cols - 1 - is_own.astype(jnp.int32))
+    pl.semaphore_wait(barrier, n_outer + n_group - 1 + n_cols - 1 - is_own.astype(jnp.int32))
     cast_start(0)
 
     loads[2].wait()
@@ -209,8 +241,8 @@
     loads[6].wait()
     fold_lower(2, through)
 
-    cast_wait(0)
-    scatter(0, mm(low[0], fetched[0]))
+    relay(0)
+    scatter(0, product(0, low.at[0]))
     slices[1] = (base1[own_rows] - summed(0)).astype(BF16)
     cast_start(1)
     carry[...] = mm(low[1], fetched[0])
@@ -222,22 +254,22 @@
     padded[...] = jnp.zeros_like(padded)
     padded[own_rows] = slices[1]
 
-    cast_wait(1)
-    scatter(1, carry[...] + mm(low[2], fetched[1]))
+    relay(1)
+    scatter(1, carry[...] + product(1, low.at[2]))
     slices[2] = (base2[own_rows] - summed(1)).astype(BF16)
     cast_start(2)
     share(2, 2)
     carry[...] = mm(uinv[1], padded[...])
 
-    cast_wait(2)
-    scatter(2, mm(upp[2], fetched[2]) - carry[...])
+    relay(2)
+    scatter(2, product(2, upp.at[2]) - carry[...])
     slices[3] = (-summed(2)).astype(BF16)
     cast_start(3)
     share(3, 1)
     carry[...] = mm(upp[1], fetched[2])
 
-    cast_wait(3)
-    scatter(3, carry[...] + mm(upp[0], fetched[3]))
+    relay(3)
+    scatter(3, carry[...] + product(3, upp.at[0]))
     slices[4] = (base0[own_rows] - summed(3)).astype(BF16)
     share(4, 0)
 
@@ -283,10 +315,13 @@
                 pltpu.VMEM((size, width), BF16),
                 pltpu.VMEM((size, size), BF16),
                 pltpu.VMEM((size, size), BF16),
+                pltpu.VMEM((size, width), F32),
                 pltpu.SemaphoreType.DMA((7,)),
                 pltpu.SemaphoreType.DMA(()),
                 pltpu.SemaphoreType.DMA((4,)),
+                pltpu.SemaphoreType.DMA((4, n_cols)),
                 pltpu.SemaphoreType.DMA((4,)),
+                pltpu.SemaphoreType.DMA((4, n_group)),
                 pltpu.SemaphoreType.DMA((4,)),
                 pltpu.SemaphoreType.DMA((4,)),
                 pltpu.SemaphoreType.DMA((3,)),

time: 70.6 us -> 69.4 us (0.983)
  Pallas kernels: 69.8 us -> 68.6 us
    pallas_call x1, Pallas kernels: 69.8 us -> 68.6 us  [body(): pl.pallas_call(functools.partial(kernel, n_rows, n_cols, n_group), out_sh...]
where the time goes in v4:
time: 69.4 us; the launch traced here: 69.3 us
  Pallas kernels  68.6 us (99%)
    pallas_call x1, Pallas kernels, body(): pl.pallas_call(functools.partial(kernel, n_rows, n_cols, n_group), out_sh...  68.6 us

profile of v4, /device:TPU:1, one launch (start us, length us, event | category | flops | bytes accessed | tf_op | source)
XLA Modules:
  0.0 69.3 jit_solution(10927332575128136588)
XLA Ops:
  0.0 68.6 %shard_map.64 = bf16[3,1,256,128]{3,2,1,0:T(8,128)(2,1)S(1)} custom-call(bf16[3,1,256,128]{3,2,1,0:T(8,128)(2,1)} %rhs_hbm.1, bf16[3,1,256,1024]{3,2,1,0:T(8,128)(2,1)} %low_hbm.1, bf16[3,1,256,1024]{3,2,1,0:T(8,128)(2,1)} %upp_hbm.1, bf16[3,1,256,256]{3,2,1,0:T(8,128)(2,1)} %linv_hbm.1, bf16[3,1,256,256]{3,2,1,0:T(8,128)(2,1)} %uinv_hbm.1, s32[3,32,32]{2,1,0:T(8,128)} %pat_hbm.1), custom_call_target="tpu_custom_call" | custom-call | tf_op jit(solution)/shard_map/pallas_call | solution.py:294
  68.6 0.7 copy.8

commit v5 on v4

--- a/solution.py
+++ b/solution.py
@@ -21,7 +21,7 @@
     rhs_hbm, low_hbm, upp_hbm, linv_hbm, uinv_hbm, pat_hbm,
     out_hbm,
     rhs, low, upp, linv, uinv, pat,
-    first, base1, base2, base0, carry, prod, land, slices, fetched, padded, n_hi, n_lo,
+    first, base1, base2, base0, carry, prod, land, slices, fetched, passing, padded, n_hi, n_lo,
     prod_f32, load_sem, pat_sem, cast_send, cast_recv, pass_send, pass_recv, sum_send, sum_recv, out_send, out_recv,
 ):
     size = rhs.shape[1]
@@ -43,21 +43,14 @@
     def across(step):
         return (owner_col + step) % n_outer * n_group + place
 
-    is_own = owner_col == col
-
-    for q in range(n_cols):
-        src_row = col * n_group + place
-
-        @pl.when(jnp.logical_or(src_row != row, q != col))
-        def _():
-            pl.semaphore_signal(barrier, inc=1, device_id=(src_row, q), device_id_type=MESH)
-
-        @pl.when(q != col)
-        def _():
-            pl.semaphore_signal(barrier, inc=1, device_id=(row, q), device_id_type=MESH)
-
-    for step in near_order:
-        pl.semaphore_signal(barrier, inc=1, device_id=(beside(step), col), device_id_type=MESH)
+
+    for step in outer_order:
+        pl.semaphore_signal(barrier, inc=1, device_id=(across(step), col), device_id_type=MESH)
+    for step in near_order + [0]:
+        for turn in range(n_cols):
+            if step or turn:
+                other = (beside(step), (col + turn) % n_cols)
+                pl.semaphore_signal(barrier, inc=1, device_id=other, device_id_type=MESH)
 
     loads = [
         pltpu.make_async_copy(linv_hbm.at[:, 0], linv, load_sem.at[0]),
@@ -74,83 +67,85 @@
 
     own_rows = pl.ds(pl.multiple_of(col * part, part), part)
 
-    block_rows = pl.ds(pl.multiple_of(place * size, size), size)
-
-    def cast_ends(rnd):
-        source = first.at[own_rows] if rnd == 0 else slices.at[rnd]
-        return source, fetched.at[rnd, pl.ds(pl.multiple_of(place * size + col * part, part), part)]
+    def cast_source(rnd):
+        return first.at[own_rows] if rnd == 0 else slices.at[rnd]
 
     def cast_copy(rnd, step):
-        source, target = cast_ends(rnd)
+        return pltpu.make_async_remote_copy(
+            src_ref=cast_source(rnd),
+            dst_ref=passing.at[rnd, owner_col],
+            send_sem=cast_send.at[rnd],
+            recv_sem=cast_recv.at[rnd, owner_col],
+            device_id=(across(step), col),
+            device_id_type=MESH,
+        )
+
+    def pass_ends(rnd, d):
+        plane = (owner_col + d) % n_outer
+        source = cast_source(rnd) if d == 0 else passing.at[rnd, plane]
+        target = fetched.at[rnd, pl.ds(pl.multiple_of(place * size + col * part, part), part)]
+        return plane, source, target
+
+    def pass_copy(rnd, d, step):
+        plane, source, target = pass_ends(rnd, d)
         return pltpu.make_async_remote_copy(
             src_ref=source,
             dst_ref=target,
-            send_sem=cast_send.at[rnd],
-            recv_sem=cast_recv.at[rnd, col],
-            device_id=(across(step), owner_col),
+            send_sem=pass_send.at[rnd],
+            recv_sem=pass_recv.at[rnd, step],
+            device_id=(beside(step), plane),
             device_id_type=MESH,
         )
+
+    def pass_on(rnd, d):
+        plane, source, target = pass_ends(rnd, d)
+        for step in near_order:
+            pass_copy(rnd, d, step).start()
+
+        @pl.when(plane != col)
+        def _():
+            pass_copy(rnd, d, 0).start()
+
+        @pl.when(plane == col)
+        def _():
+            pltpu.make_async_copy(source, target, pass_recv.at[rnd, 0]).start()
 
     def cast_start(rnd):
         for step in outer_order:
             cast_copy(rnd, step).start()
-
-        @pl.when(jnp.logical_not(is_own))
-        def _():
-            cast_copy(rnd, 0).start()
-
-        @pl.when(is_own)
-        def _():
-            source, target = cast_ends(rnd)
-            pltpu.make_async_copy(source, target, cast_recv.at[rnd, col]).start()
-
-    def pass_copy(rnd, chip, step):
-        rows = fetched.at[rnd, pl.ds(pl.multiple_of(place * size + chip * 2 * part, part), 2 * part)]
-        return pltpu.make_async_remote_copy(
-            src_ref=rows,
-            dst_ref=rows,
-            send_sem=pass_send.at[rnd],
-            recv_sem=pass_recv.at[rnd, step],
-            device_id=(beside(step), col),
-            device_id_type=MESH,
-        )
-
-    def chip_at(d):
-        return (col // 2 + d) % (n_cols // 2)
+        pass_on(rnd, 0)
 
     def relay(rnd):
-        for d in (0, 1, 3, 2):
-            chip = chip_at(d)
-            for k in range(2):
-                q = chip * 2 + k
-                rows = fetched.at[rnd, pl.ds(pl.multiple_of(place * size + q * part, part), part)]
-                pltpu.make_async_copy(rows, rows, cast_recv.at[rnd, q]).wait()
-            for step in near_order:
-                pass_copy(rnd, chip, step).start()
+        for d in (1, 7, 2, 6, 3, 5, 4):
+            plane, source, target = pass_ends(rnd, d)
+            pltpu.make_async_copy(source, source, cast_recv.at[rnd, plane]).wait()
+            pass_on(rnd, d)
 
     def product(rnd, matrix):
         def piece(offset):
             where = pl.ds(pl.multiple_of((place + offset) % n_group * size, size), size)
             return mm(matrix[:, where], fetched[rnd, where])
 
-        prod_f32[...] = piece(0)
-        for step in (1, 3, 2):
+        for step in (0, 1, 3, 2):
             where = pl.ds(pl.multiple_of((place + n_group - step) % n_group * size, size), size)
             pltpu.make_async_copy(fetched.at[rnd, where], fetched.at[rnd, where], pass_recv.at[rnd, step]).wait()
-            prod_f32[...] += piece(n_group - step)
+            if step:
+                prod_f32[...] += piece(n_group - step)
+            else:
+                prod_f32[...] = piece(0)
         return prod_f32[...]
 
     def cast_drain(rnd):
         for step in outer_order:
             cast_copy(rnd, step).wait_send()
-
-        @pl.when(jnp.logical_not(is_own))
-        def _():
-            cast_copy(rnd, 0).wait_send()
-
-        for d in range(n_cols // 2):
+        for d in range(n_outer):
+            plane, source, target = pass_ends(rnd, d)
             for step in near_order:
                 pass_copy(rnd, d, step).wait_send()
+
+            @pl.when(plane != col)
+            def _():
+                pass_copy(rnd, d, 0).wait_send()
 
     def peer(step):
         return lax.rem(col + step, n_cols)
@@ -219,7 +214,7 @@
     loads[1].wait()
     first[...] = mm(linv[0], rhs[0]).astype(BF16)
 
-    pl.semaphore_wait(barrier, n_outer + n_group - 1 + n_cols - 1 - is_own.astype(jnp.int32))
+    pl.semaphore_wait(barrier, n_outer - 1 + n_group * n_cols - 1)
     cast_start(0)
 
     loads[2].wait()
@@ -312,6 +307,7 @@
                 pltpu.VMEM((4, n_cols, part, width), BF16),
                 pltpu.VMEM((5, part, width), BF16),
                 pltpu.VMEM((4, span, width), BF16),
+                pltpu.VMEM((4, n_rows // n_group, part, width), BF16),
                 pltpu.VMEM((size, width), BF16),
                 pltpu.VMEM((size, size), BF16),
                 pltpu.VMEM((size, size), BF16),
@@ -319,7 +315,7 @@
                 pltpu.SemaphoreType.DMA((7,)),
                 pltpu.SemaphoreType.DMA(()),
                 pltpu.SemaphoreType.DMA((4,)),
-                pltpu.SemaphoreType.DMA((4, n_cols)),
+                pltpu.SemaphoreType.DMA((4, n_rows // n_group)),
                 pltpu.SemaphoreType.DMA((4,)),
                 pltpu.SemaphoreType.DMA((4, n_group)),
                 pltpu.SemaphoreType.DMA((4,)),

time: 69.4 us -> 68.9 us (level)
  no operation moved by 1% of the time
where the time goes in v5:
time: 68.9 us
  Pallas kernels  68.2 us (99%)
    pallas_call x1, Pallas kernels, body(): pl.pallas_call(functools.partial(kernel, n_rows, n_cols, n_group), out_sh...  68.2 us

profile of v5, /device:TPU:1, one launch (start us, length us, event | category | flops | bytes accessed | tf_op | source)
XLA Modules:
  0.0 68.9 jit_solution(12725734884153689019)
XLA Ops:
  0.0 68.2 %shard_map.64 = bf16[3,1,256,128]{3,2,1,0:T(8,128)(2,1)S(1)} custom-call(bf16[3,1,256,128]{3,2,1,0:T(8,128)(2,1)} %rhs_hbm.1, bf16[3,1,256,1024]{3,2,1,0:T(8,128)(2,1)} %low_hbm.1, bf16[3,1,256,1024]{3,2,1,0:T(8,128)(2,1)} %upp_hbm.1, bf16[3,1,256,256]{3,2,1,0:T(8,128)(2,1)} %linv_hbm.1, bf16[3,1,256,256]{3,2,1,0:T(8,128)(2,1)} %uinv_hbm.1, s32[3,32,32]{2,1,0:T(8,128)} %pat_hbm.1), custom_call_target="tpu_custom_call" | custom-call | tf_op jit(solution)/shard_map/pallas_call | solution.py:289
  68.2 0.7 copy.8

commit v6 on v2

v6 whole, which is shorter than its diff:
```python
import functools

import jax
import jax.numpy as jnp
from jax import lax
from jax.experimental import pallas as pl
from jax.experimental.pallas import tpu as pltpu
from jax.sharding import PartitionSpec as P

MESH = pl.DeviceIdType.MESH
F32 = jnp.float32
BF16 = jnp.bfloat16
HALVES = 2
SUM_TYPE = BF16


def mm(a, b):
    return jnp.dot(a, b, preferred_element_type=F32)


def mm_t(a, b):
    return lax.dot_general(a, b, (((1,), (1,)), ((), ())), preferred_element_type=F32)


def kernel(
    n_rows, n_cols, n_group,
    rhs_hbm, low_hbm, upp_hbm, linv_hbm, uinv_hbm, pat_hbm,
    out_hbm,
    rhs, low, upp, linv, uinv, pat, low_t, upp_t,
    first, base1, base2, base0, base3, carry, prod, land, slices, fetched, n_hi, n_lo,
    load_sem, pat_sem, cast_send, cast_recv, sum_send, sum_recv, out_send, out_recv,
):
    size = rhs.shape[1]
    width = rhs.shape[2]
    part = width // n_cols
    n_chips = n_cols // HALVES
    half_rows = width // HALVES
    row = lax.axis_index("prow")
    col = lax.axis_index("pcol")
    core = lax.rem(col, HALVES)
    chip = col // HALVES
    owner_col = row // n_group
    place = row % n_group
    n_outer = n_rows // n_group
    is_own = owner_col == col

    barrier = pltpu.get_barrier_semaphore()
    for q in range(n_cols):
        for b in range(n_group):
            src_row = col * n_group + b

            @pl.when(jnp.logical_or(src_row != row, q != col))
            def _():
                pl.semaphore_signal(barrier, inc=1, device_id=(src_row, q), device_id_type=MESH)

        @pl.when(q != col)
        def _():
            pl.semaphore_signal(barrier, inc=1, device_id=(row, q), device_id_type=MESH)

    loads = [
        pltpu.make_async_copy(linv_hbm.at[:, 0], linv, load_sem.at[0]),
        pltpu.make_async_copy(rhs_hbm.at[:, 0], rhs, load_sem.at[1]),
        pltpu.make_async_copy(pat_hbm, pat, pat_sem),
        pltpu.make_async_copy(low_hbm.at[0, 0], low.at[0], load_sem.at[2]),
        pltpu.make_async_copy(uinv_hbm.at[:, 0], uinv, load_sem.at[3]),
        pltpu.make_async_copy(low_hbm.at[1, 0], low.at[1], load_sem.at[4]),
        pltpu.make_async_copy(low_hbm.at[2, 0], low.at[2], load_sem.at[5]),
        pltpu.make_async_copy(upp_hbm.at[:, 0], upp, load_sem.at[6]),
    ]
    for copy in loads:
        copy.start()

    own = pl.ds(pl.multiple_of(core * half_rows + chip * part, part), part)
    in_half = pl.ds(pl.multiple_of(chip * part, part), part)
    in_span = pl.ds(pl.multiple_of(place * size, size), size)

    def target_row(step):
        i, j = step // n_group, step % n_group
        d_outer = n_outer // 2 + ((i + 1) // 2) * (1 - 2 * (i % 2))
        d_inner = n_group // 2 + ((j + 1) // 2) * (1 - 2 * (j % 2))
        outer = (row // n_group + d_outer) % n_outer
        inner = (row % n_group + d_inner) % n_group
        return outer * n_group + inner

    def cast_ends(rnd):
        source = first.at[own] if rnd == 0 else slices.at[rnd]
        return source, fetched.at[rnd, core, in_half, in_span]

    def cast_copy(rnd, step):
        source, target = cast_ends(rnd)
        return pltpu.make_async_remote_copy(
            src_ref=source,
            dst_ref=target,
            send_sem=cast_send.at[rnd],
            recv_sem=cast_recv.at[rnd, core],
            device_id=(target_row(step), owner_col),
            device_id_type=MESH,
        )

    def cast_start(rnd):
        def one(step, unused):
            cast_copy(rnd, step).start()
            return unused

        lax.fori_loop(0, n_rows - 1, one, 0)

        @pl.when(jnp.logical_not(is_own))
        def _():
            cast_copy(rnd, n_rows - 1).start()

        @pl.when(is_own)
        def _():
            source, target = cast_ends(rnd)
            pltpu.make_async_copy(source, target, cast_recv.at[rnd, core]).start()

    def cast_wait(rnd, half):
        whole = fetched.at[rnd, half]
        pltpu.make_async_copy(whole, whole, cast_recv.at[rnd, half]).wait()

    def cast_drain(rnd):
        def one(step, unused):
            cast_copy(rnd, step).wait_send()
            return unused

        lax.fori_loop(0, n_rows - 1, one, 0)

        @pl.when(jnp.logical_not(is_own))
        def _():
            cast_copy(rnd, n_rows - 1).wait_send()

    def sum_copy(rnd, half, other):
        return pltpu.make_async_remote_copy(
            src_ref=prod.at[rnd, half, pl.ds(pl.multiple_of(other * part, part), part)],
            dst_ref=land.at[rnd, col],
            send_sem=sum_send.at[rnd, half],
            recv_sem=sum_recv.at[rnd],
            device_id=(row, other * HALVES + half),
            device_id_type=MESH,
        )

    chip_order = [n_chips // 2] + [d for d in range(1, n_chips) if d != n_chips // 2]

    def scatter(rnd, half, value):
        prod[rnd, half] = value.astype(prod.dtype)
        for step in chip_order:
            sum_copy(rnd, half, lax.rem(chip + step, n_chips)).start()

        @pl.when(core != half)
        def _():
            sum_copy(rnd, half, chip).start()

    def scatter_drain(rnd, half):
        for step in chip_order:
            sum_copy(rnd, half, lax.rem(chip + step, n_chips)).wait_send()

        @pl.when(core != half)
        def _():
            sum_copy(rnd, half, chip).wait_send()

    def summed(rnd, half):
        land[rnd, col] = prod[rnd, half, in_half]
        most = land.at[rnd, pl.ds(0, n_cols - 1)]
        pltpu.make_async_copy(most, most, sum_recv.at[rnd]).wait()
        total = land[rnd, 0].astype(F32)
        for q in range(1, n_cols):
            total = total + land[rnd, q].astype(F32)
        return total

    def out_copy(rnd, level, step):
        return pltpu.make_async_remote_copy(
            src_ref=slices.at[rnd],
            dst_ref=out_hbm.at[level, own],
            send_sem=out_send.at[level],
            recv_sem=out_recv.at[level],
            device_id=(row, lax.rem(col + step, n_cols)),
            device_id_type=MESH,
        )

    peer_order = [4, 3, 5, 2, 6, 1, 7]

    def share(rnd, level):
        for step in peer_order:
            out_copy(rnd, level, step).start()
        pltpu.make_async_copy(slices.at[rnd], out_hbm.at[level, own], out_recv.at[level]).start()

    def share_wait(rnd, level):
        whole = out_hbm.at[level]
        pltpu.make_async_copy(whole, whole, out_recv.at[level]).wait()
        for step in peer_order:
            out_copy(rnd, level, step).wait_send()

    def fold_lower(pair, products):
        for b in range(n_group):
            cols = slice(b * size, (b + 1) * size)
            keep = pat[pair, row, col * n_group + b].astype(F32)
            low_t[pair, cols] = (products(low[pair, :, cols]) * keep).T.astype(BF16)

    def fold_upper(pair, level):
        for b in range(n_group):
            cols = slice(b * size, (b + 1) * size)
            keep = pat[pair, col * n_group + b, row].astype(F32)
            upp_t[pair, cols] = (mm(uinv[level], upp[pair, :, cols]) * keep).T.astype(BF16)

    loads[0].wait()
    loads[1].wait()
    first[...] = mm(linv[0], rhs[0]).T.astype(BF16)

    pl.semaphore_wait(barrier, n_rows + n_cols - 1 - is_own.astype(jnp.int32))

    @pl.when(core == 0)
    def _():
        cast_start(0)

    loads[2].wait()
    loads[3].wait()
    fold_lower(0, lambda block: mm(linv[1], block))
    base1[...] = mm(linv[1], rhs[1]).T
    loads[4].wait()
    both = mm(uinv[2], linv[2])
    n_hi[...] = both.astype(BF16)
    n_lo[...] = (both - n_hi[...].astype(F32)).astype(BF16)

    def through(block):
        return mm(n_hi[...], block) + mm(n_lo[...], block)

    base2[...] = through(rhs[2]).T
    base0[...] = mm_t(first[...], uinv[0])

    loads[5].wait()
    fold_lower(1, through)
    loads[6].wait()
    fold_lower(2, through)
    loads[7].wait()
    fold_upper(2, 1)
    fold_upper(1, 0)
    fold_upper(0, 0)

    @pl.when(core == 1)
    def _():
        cast_start(0)

    for rnd in range(4):
        for half in range(HALVES):
            cast_wait(rnd, half)
            got = fetched[rnd, half]
            if rnd == 0:
                value = mm(got, low_t[0])
            elif rnd == 1:
                value = mm(got, low_t[2]) + carry[half]
            elif rnd == 2:
                value = mm(got, upp_t[2])
            else:
                value = mm(got, upp_t[0]) + carry[half]
            scatter(rnd, half, value)
            if rnd == 0:
                carry[half] = mm(got, low_t[1])
            if rnd == 2:
                carry[half] = mm(got, upp_t[1])

            @pl.when(core == half)
            def _():
                base = (lambda: base1[own], lambda: base2[own], lambda: base3[...], lambda: base0[own])[rnd]()
                slices[rnd + 1] = (base - summed(rnd, half)).astype(BF16)
                if rnd < 3:
                    cast_start(rnd + 1)
                if rnd == 0:
                    base3[...] = mm_t(slices[1], uinv[1])
                else:
                    share(rnd + 1, 3 - rnd)

    for rnd in range(4):
        cast_drain(rnd)
        for half in range(HALVES):
            scatter_drain(rnd, half)
    for rnd in range(1, 4):
        share_wait(rnd + 1, 3 - rnd)


def solution(mesh):
    n_rows, n_cols = mesh.shape["prow"], mesh.shape["pcol"]

    def body(right_side, lower_blocks, upper_blocks, lower_inverse, upper_inverse, pattern):
        levels, _, size, width = right_side.shape
        pairs, _, _, span = lower_blocks.shape
        n_group = span // size
        part = width // n_cols
        half_rows = width // HALVES
        any_spec = pl.BlockSpec(memory_space=pl.ANY)
        turned = pl.pallas_call(
            functools.partial(kernel, n_rows, n_cols, n_group),
            out_shape=jax.ShapeDtypeStruct((levels, width, size), BF16),
            in_specs=[any_spec] * 6,
            out_specs=any_spec,
            scratch_shapes=[
                pltpu.VMEM((levels, size, width), BF16),
                pltpu.VMEM((pairs, size, span), BF16),
                pltpu.VMEM((pairs, size, span), BF16),
                pltpu.VMEM((levels, size, size), BF16),
                pltpu.VMEM((levels, size, size), BF16),
                pltpu.SMEM(pattern.shape, jnp.int32),
                pltpu.VMEM((pairs, span, size), BF16),
                pltpu.VMEM((pairs, span, size), BF16),
                pltpu.VMEM((width, size), BF16),
                pltpu.VMEM((width, size), F32),
                pltpu.VMEM((width, size), F32),
                pltpu.VMEM((width, size), F32),
                pltpu.VMEM((part, size), F32),
                pltpu.VMEM((HALVES, half_rows, size), F32),
                pltpu.VMEM((4, HALVES, half_rows, size), SUM_TYPE),
                pltpu.VMEM((4, n_cols, part, size), SUM_TYPE),
                pltpu.VMEM((5, part, size), BF16),
                pltpu.VMEM((4, HALVES, half_rows, span), BF16),
                pltpu.VMEM((size, size), BF16),
                pltpu.VMEM((size, size), BF16),
                pltpu.SemaphoreType.DMA((7,)),
                pltpu.SemaphoreType.DMA(()),
                pltpu.SemaphoreType.DMA((4,)),
                pltpu.SemaphoreType.DMA((4, HALVES)),
                pltpu.SemaphoreType.DMA((4, HALVES)),
                pltpu.SemaphoreType.DMA((4,)),
                pltpu.SemaphoreType.DMA((3,)),
                pltpu.SemaphoreType.DMA((3,)),
            ],
            compiler_params=pltpu.CompilerParams(collective_id=0, has_side_effects=True, vmem_limit_bytes=24 * 1024 * 1024),
        )(*[pltpu.with_memory_space_constraint(x, pltpu.HBM) for x in (right_side, lower_blocks, upper_blocks, lower_inverse, upper_inverse, pattern)])
        return jnp.swapaxes(turned, 1, 2)[:, None]

    placed = (
        P(None, "prow", None, None),
        P(None, "prow", None, "pcol"),
        P(None, "prow", None, "pcol"),
        P(None, "prow", None, None),
        P(None, "prow", None, None),
        P(),
    )
    return jax.shard_map(
        body, mesh=mesh, in_specs=placed, out_specs=P(None, "prow", None, None), check_vma=False
    )
```

time: 70.9 us -> 67.8 us (0.956)
  Pallas kernels: 70.1 us -> 66.9 us
    pallas_call x1, Pallas kernels: 70.1 us -> 66.9 us  [body(): pl.pallas_call(functools.partial(kernel, n_rows, n_cols, n_group), out_sh...]
    broadcast_in_dim x0 -> x1, local copies, waits for them, and re-layouts: none -> 0.82 us  [body(): return jnp.swapaxes(turned, 1, 2)[:, None]]
where the time goes in v6:
time: 67.8 us; the launch traced here: 67.7 us
  Pallas kernels  66.9 us (99%)
  local copies, waits for them, and re-layouts  0.82 us (1%)
    pallas_call x1, Pallas kernels, body(): pl.pallas_call(functools.partial(kernel, n_rows, n_cols, n_group), out_sh...  66.9 us

profile of v6, /device:TPU:1, one launch (start us, length us, event | category | flops | bytes accessed | tf_op | source)
XLA Modules:
  0.0 67.7 jit_solution(10210287611724951184)
XLA Ops:
  0.0 66.9 %shard_map.64 = bf16[3,128,256]{2,1,0:T(8,128)(2,1)S(1)} custom-call(bf16[3,1,256,128]{3,2,1,0:T(8,128)(2,1)} %rhs_hbm.1, bf16[3,1,256,1024]{3,2,1,0:T(8,128)(2,1)} %low_hbm.1, bf16[3,1,256,1024]{3,2,1,0:T(8,128)(2,1)} %upp_hbm.1, bf16[3,1,256,256]{3,2,1,0:T(8,128)(2,1)} %linv_hbm.1, bf16[3,1,256,256]{3,2,1,0:T(8,128)(2,1)} %uinv_hbm.1, s32[3,32,32]{2,1,0:T(8,128)} %pat_hbm.1), custom_call_target="tpu_custom_call" | custom-call | tf_op jit(solution)/shard_map/pallas_call | solution.py:289
  66.9 0.8 %copy.7 = bf16[3,1,256,128]{3,2,1,0:T(8,128)(2,1)} copy(bf16[3,1,256,128]{2,3,0,1:T(8,128)(2,1)S(1)} %bitcast.3) | data formatting | bytes 393216 | tf_op jit(solution)/shard_map/broadcast_in_dim | solution.py:326

commit v7 on v6

--- a/solution.py
+++ b/solution.py
@@ -72,7 +72,6 @@
 
     own = pl.ds(pl.multiple_of(core * half_rows + chip * part, part), part)
     in_half = pl.ds(pl.multiple_of(chip * part, part), part)
-    in_span = pl.ds(pl.multiple_of(place * size, size), size)
 
     def target_row(step):
         i, j = step // n_group, step % n_group
@@ -84,7 +83,7 @@
 
     def cast_ends(rnd):
         source = first.at[own] if rnd == 0 else slices.at[rnd]
-        return source, fetched.at[rnd, core, in_half, in_span]
+        return source, fetched.at[rnd, core, place, in_half]
 
     def cast_copy(rnd, step):
         source, target = cast_ends(rnd)
@@ -102,7 +101,8 @@
             cast_copy(rnd, step).start()
             return unused
 
-        lax.fori_loop(0, n_rows - 1, one, 0)
+        for step in range(n_rows - 1):
+            one(step, 0)
 
         @pl.when(jnp.logical_not(is_own))
         def _():
@@ -242,7 +242,7 @@
     for rnd in range(4):
         for half in range(HALVES):
             cast_wait(rnd, half)
-            got = fetched[rnd, half]
+            got = jnp.concatenate([fetched[rnd, half, b] for b in range(n_group)], axis=1)
             if rnd == 0:
                 value = mm(got, low_t[0])
             elif rnd == 1:
@@ -309,7 +309,7 @@
                 pltpu.VMEM((4, HALVES, half_rows, size), SUM_TYPE),
                 pltpu.VMEM((4, n_cols, part, size), SUM_TYPE),
                 pltpu.VMEM((5, part, size), BF16),
-                pltpu.VMEM((4, HALVES, half_rows, span), BF16),
+                pltpu.VMEM((4, HALVES, n_group, half_rows, size), BF16),
                 pltpu.VMEM((size, size), BF16),
                 pltpu.VMEM((size, size), BF16),
                 pltpu.SemaphoreType.DMA((7,)),

time: 67.8 us -> 66.8 us (0.985)
  Pallas kernels: 66.9 us -> 65.9 us
    pallas_call x1, Pallas kernels: 66.9 us -> 65.9 us  [body(): pl.pallas_call(functools.partial(kernel, n_rows, n_cols, n_group), out_sh...]
where the time goes in v7:
time: 66.8 us; the launch traced here: 66.7 us
  Pallas kernels  65.9 us (99%)
  local copies, waits for them, and re-layouts  0.82 us (1%)
    pallas_call x1, Pallas kernels, body(): pl.pallas_call(functools.partial(kernel, n_rows, n_cols, n_group), out_sh...  65.9 us

profile of v7, /device:TPU:1, one launch (start us, length us, event | category | flops | bytes accessed | tf_op | source)
XLA Modules:
  0.0 66.7 jit_solution(6417634057774452541)
XLA Ops:
  0.0 65.9 %shard_map.64 = bf16[3,128,256]{2,1,0:T(8,128)(2,1)S(1)} custom-call(bf16[3,1,256,128]{3,2,1,0:T(8,128)(2,1)} %rhs_hbm.1, bf16[3,1,256,1024]{3,2,1,0:T(8,128)(2,1)} %low_hbm.1, bf16[3,1,256,1024]{3,2,1,0:T(8,128)(2,1)} %upp_hbm.1, bf16[3,1,256,256]{3,2,1,0:T(8,128)(2,1)} %linv_hbm.1, bf16[3,1,256,256]{3,2,1,0:T(8,128)(2,1)} %uinv_hbm.1, s32[3,32,32]{2,1,0:T(8,128)} %pat_hbm.1), custom_call_target="tpu_custom_call" | custom-call | tf_op jit(solution)/shard_map/pallas_call | solution.py:289
  65.9 0.8 %copy.7 = bf16[3,1,256,128]{3,2,1,0:T(8,128)(2,1)} copy(bf16[3,1,256,128]{2,3,0,1:T(8,128)(2,1)S(1)} %bitcast.3) | data formatting | bytes 393216 | tf_op jit(solution)/shard_map/broadcast_in_dim | solution.py:326

commit v8 on v7

--- a/solution.py
+++ b/solution.py
@@ -252,10 +252,6 @@
             else:
                 value = mm(got, upp_t[0]) + carry[half]
             scatter(rnd, half, value)
-            if rnd == 0:
-                carry[half] = mm(got, low_t[1])
-            if rnd == 2:
-                carry[half] = mm(got, upp_t[1])
 
             @pl.when(core == half)
             def _():
@@ -267,6 +263,11 @@
                     base3[...] = mm_t(slices[1], uinv[1])
                 else:
                     share(rnd + 1, 3 - rnd)
+
+            if rnd == 0:
+                carry[half] = mm(got, low_t[1])
+            if rnd == 2:
+                carry[half] = mm(got, upp_t[1])
 
     for rnd in range(4):
         cast_drain(rnd)

time: 66.8 us -> 66.5 us (level)
  no operation moved by 1% of the time
where the time goes in v8:
time: 66.5 us; the launch traced here: 66.4 us
  Pallas kernels  65.6 us (99%)
  local copies, waits for them, and re-layouts  0.82 us (1%)
    pallas_call x1, Pallas kernels, body(): pl.pallas_call(functools.partial(kernel, n_rows, n_cols, n_group), out_sh...  65.6 us

profile of v8, /device:TPU:1, one launch (start us, length us, event | category | flops | bytes accessed | tf_op | source)
XLA Modules:
  0.0 66.4 jit_solution(6028843045377730970)
XLA Ops:
  0.0 65.6 %shard_map.64 = bf16[3,128,256]{2,1,0:T(8,128)(2,1)S(1)} custom-call(bf16[3,1,256,128]{3,2,1,0:T(8,128)(2,1)} %rhs_hbm.1, bf16[3,1,256,1024]{3,2,1,0:T(8,128)(2,1)} %low_hbm.1, bf16[3,1,256,1024]{3,2,1,0:T(8,128)(2,1)} %upp_hbm.1, bf16[3,1,256,256]{3,2,1,0:T(8,128)(2,1)} %linv_hbm.1, bf16[3,1,256,256]{3,2,1,0:T(8,128)(2,1)} %uinv_hbm.1, s32[3,32,32]{2,1,0:T(8,128)} %pat_hbm.1), custom_call_target="tpu_custom_call" | custom-call | tf_op jit(solution)/shard_map/pallas_call | solution.py:290
  65.6 0.8 %copy.7 = bf16[3,1,256,128]{3,2,1,0:T(8,128)(2,1)} copy(bf16[3,1,256,128]{2,3,0,1:T(8,128)(2,1)S(1)} %bitcast.3) | data formatting | bytes 393216 | tf_op jit(solution)/shard_map/broadcast_in_dim | solution.py:327
